TPU v7x, 1024 devices: a whole 8x8x8 slice. The times are simulated.
1024 devices in a mesh: gx: 16 (over y, core), yz: 64 (over x, z).
Axes of the slice: x: 8, y: 8, z: 8, core: 2. Of those that a mesh axis runs over, the one named last changes fastest.
Arguments:
- gas: float32 [10, 32, 256, 128], P(None, 'gx', 'yz'), may hold values from -6 to 6
- kappa: float32 [32, 256, 128], P('gx', 'yz'), may hold values from 0.01 to 0.06
- velocity: float32 [32, 256, 128], P('gx', 'yz'), may hold values from 0.1 to 0.6
- drop_mass: float32 [32768, 128], P(('gx', 'yz')), may hold values from 0.2 to 2
- drop_temp: float32 [32768, 128], P(('gx', 'yz')), may hold values from -6 to 6
- block_fill: int32 [32768], P(('gx', 'yz')), may hold values from 1 to 128
- drop_cell: int32 [32768, 128], P(('gx', 'yz')), may hold values from 0 to 1023
- block_dest: int32 [32768, 1], P(('gx', 'yz')), may hold values from 0 to 63; in each aligned block of 32 rows (0 to 31, 32 to 63, ...) at most 2 rows name the same one
Outputs:
- gas_next: float32 [10, 32, 256, 128], P(None, 'gx', 'yz')
- mass_next: float32 [32768, 128], P(('gx', 'yz'))
- temp_next: float32 [32768, 128], P(('gx', 'yz'))
Inputs may be any that keep to these rules, and one draw needn't show every extreme that they name: `block_dest`: among the blocks of one device, at most 2 name the same brick, and in every draw some device sends exactly 2 blocks to some brick.
All inputs are finite; a program needn't handle non-finite values.
Results may differ from a plain program's by a relative error of at most 0.00007.
Values sent between devices are 32-bit elements; how exact they have to be, the bound alone decides.
A program may use at most 32 MiB of HBM per device.

v0:
```python
import math

import jax
import jax.numpy as jnp
from jax import lax
from jax.sharding import PartitionSpec as P

SUBSTEPS = 4


evap_coef = 0.3
heat_coef = 0.8
latent_coef = 0.5
drop_dt = 0.25
lane_width = 128
block_rows = 2048


def with_halo(cells, sides, width):
    for axis, dim in sides:
        count = lax.axis_size(axis)
        ends = count - 1
        head = lax.slice_in_dim(cells, 0, width, axis=dim)
        tail = lax.slice_in_dim(cells, cells.shape[dim] - width, cells.shape[dim], axis=dim)
        cells = jnp.concatenate(
            [
                lax.ppermute(tail, axis, [(i, (i + 1) % count) for i in range(ends)]),
                cells,
                lax.ppermute(head, axis, [((i + 1) % count, i) for i in range(ends)]),
            ],
            axis=dim,
        )
    return cells


def droplet_step(mass_now, temp_now, fuel_gas, temp_gas, living):
    src_mass = jnp.zeros_like(mass_now)
    src_energy = jnp.zeros_like(mass_now)
    for substep in range(SUBSTEPS):
        evap_rate = evap_coef * jax.nn.softplus(temp_now - fuel_gas)
        heat_flow = heat_coef * (temp_gas - temp_now)
        shrunk = mass_now * jnp.exp(-drop_dt * evap_rate)
        src_mass = src_mass + (mass_now - shrunk)
        src_energy = src_energy - drop_dt * heat_flow * mass_now
        temp_now = temp_now + drop_dt * (heat_flow - latent_coef * evap_rate)
        mass_now = shrunk
    zero = jnp.zeros_like(mass_now)
    return (
        jnp.where(living, mass_now, zero),
        jnp.where(living, temp_now, zero),
        jnp.where(living, src_mass, zero),
        jnp.where(living, src_energy, zero),
    )


def split_tables(cell_ids, upper_count):
    lower_ids = jnp.arange(lane_width, dtype=jnp.int32)
    upper_ids = jnp.arange(upper_count, dtype=jnp.int32)
    upper = cell_ids // lane_width
    lower = cell_ids - upper * lane_width
    valid = cell_ids >= 0
    lower_hot = ((lower[:, None] == lower_ids[None, :]) & valid[:, None]).astype(jnp.float32)
    upper_hot = ((upper[:, None] == upper_ids[None, :]) & valid[:, None]).astype(jnp.float32)
    return (lower_hot, upper_hot)


def body(gas, kappa, velocity, drop_mass, drop_temp, block_fill, drop_cell, block_dest):
    nfield, brick_x, brick_y, brick_z = gas.shape
    cell_count = brick_x * brick_y * brick_z
    upper_count = cell_count // lane_width
    peer_count = lax.axis_size("yz")
    blocks = drop_mass.shape[0]
    per_block = drop_mass.shape[1]
    capacity = max(2, 2 * blocks // peer_count)
    lane_ids = jnp.arange(per_block, dtype=jnp.int32)
    living = lane_ids[None, :] < block_fill[:, None]
    target = block_dest[:, 0]
    member = (target[:, None] == jnp.arange(peer_count, dtype=jnp.int32)[None, :]).astype(jnp.int32)
    before = jnp.cumsum(member, axis=0) - member
    ranking = jnp.sum(before * member, axis=1)
    slot_index = target * capacity + ranking
    sent_cell = jnp.where(living, drop_cell, -1)

    def to_slots(values, filler):
        empty = jnp.full((peer_count * capacity, per_block), filler, values.dtype)
        return empty.at[slot_index].set(values).reshape(peer_count, capacity, per_block)

    def from_slots(values):
        return values.reshape(-1, per_block)[slot_index]

    fuel_table = gas[0].reshape(upper_count, lane_width).T
    temp_table = gas[nfield - 1].reshape(upper_count, lane_width).T
    both_tables = jnp.concatenate([fuel_table, temp_table], axis=1)
    cell_ids = lax.all_to_all(
        to_slots(sent_cell, -1), "yz", split_axis=0, concat_axis=0, tiled=True
    )
    flat_ids = cell_ids.reshape(-1)
    total = flat_ids.shape[0]
    step = math.gcd(total, block_rows)

    def one_block(ids):
        lower_hot, upper_hot = split_tables(ids, upper_count)
        picked = jnp.dot(
            lower_hot,
            both_tables,
            precision=lax.Precision.HIGHEST,
            preferred_element_type=jnp.float32,
        )
        fuel_part = jnp.sum(picked[:, :upper_count] * upper_hot, axis=1)
        temp_part = jnp.sum(picked[:, upper_count:] * upper_hot, axis=1)
        return (fuel_part, temp_part)

    fuel_gas, temp_gas = lax.map(one_block, flat_ids.reshape(total // step, step))
    fuel_gas, temp_gas = (fuel_gas.reshape(cell_ids.shape), temp_gas.reshape(cell_ids.shape))
    fuel_back = lax.all_to_all(fuel_gas, "yz", split_axis=0, concat_axis=0, tiled=True)
    temp_back = lax.all_to_all(temp_gas, "yz", split_axis=0, concat_axis=0, tiled=True)
    mass_next, temp_next, src_mass, src_energy = droplet_step(
        drop_mass, drop_temp, from_slots(fuel_back), from_slots(temp_back), living
    )
    mass_recv, energy_recv = (
        lax.all_to_all(to_slots(src_mass, 0.0), "yz", split_axis=0, concat_axis=0, tiled=True),
        lax.all_to_all(to_slots(src_energy, 0.0), "yz", split_axis=0, concat_axis=0, tiled=True),
    )
    flat_ids = cell_ids.reshape(-1)
    total = flat_ids.shape[0]
    step = math.gcd(total, block_rows)

    def add_block(summed, pieces):
        ids, mass_part, energy_part = pieces
        lower_hot, upper_hot = split_tables(ids, upper_count)
        weighted = jnp.concatenate(
            [upper_hot * mass_part[:, None], upper_hot * energy_part[:, None]], axis=1
        )
        term = lax.dot_general(
            weighted,
            lower_hot,
            (((0,), (0,)), ((), ())),
            precision=lax.Precision.HIGHEST,
            preferred_element_type=jnp.float32,
        )
        return (summed + term, None)

    start = jnp.zeros((2 * upper_count, lane_width), jnp.float32)
    summed, unused = lax.scan(
        add_block,
        start,
        (flat_ids.reshape(-1, step), mass_recv.reshape(-1, step), energy_recv.reshape(-1, step)),
    )
    sources = summed.reshape(2, brick_x, brick_y, brick_z)
    padded = with_halo(gas, (("gx", 1), ("yz", 2)), 1)
    center = padded[:, 1:-1, 1:-1]
    edged = jnp.concatenate([gas[:, :, :, :1], gas, gas[:, :, :, -1:]], axis=3)
    beside_all = (
        padded[:, 2:, 1:-1] + padded[:, :-2, 1:-1] + padded[:, 1:-1, 2:] + padded[:, 1:-1, :-2]
    )
    beside_all = beside_all + edged[:, :, :, 2:] + edged[:, :, :, :-2]
    transported = (
        center
        + kappa[None] * (beside_all - 6.0 * center)
        - velocity[None] * (center - padded[:, :-2, 1:-1])
    )
    gas_next = transported.at[0].add(sources[0])
    gas_next = gas_next.at[nfield - 1].add(sources[1])
    return (gas_next, mass_next, temp_next)


def solution(mesh):
    in_specs = (
        P(None, "gx", "yz", None),
        P("gx", "yz", None),
        P("gx", "yz", None),
        P(("gx", "yz"), None),
        P(("gx", "yz"), None),
        P(("gx", "yz")),
        P(("gx", "yz"), None),
        P(("gx", "yz"), None),
    )
    out_specs = (P(None, "gx", "yz", None), P(("gx", "yz"), None), P(("gx", "yz"), None))
    return jax.shard_map(body, mesh=mesh, in_specs=in_specs, out_specs=out_specs, check_vma=False)
```

profile of v0, /device:TPU:64, one launch (start us, length us, event | category | flops | bytes accessed | tf_op | source)
XLA Modules:
  0.0 146.2 jit_solution(1526020758204051407)
XLA Ops:
  0.6 0.6 copy-done.8
  1.4 0.2 select_reduce_fusion
  1.6 0.5 copy-done.4
  2.1 0.1 copy-done.5
  2.3 1.3 scatter_custom_fusion
  3.6 22.7 %all-to-all-start = ((s32[64,2,128]{2,1,0:T(2,128)}), s32[64,2,128]{2,1,0:T(2,128)S(1)}, u32[]{:S(2)}, u32[]{:S(2)}) async-start(s32[64,2,128]{2,1,0:T(2,128)} %bitcast.6), calls=%async_computation | async-start | bytes 131072 | tf_op jit(solution)/shard_map/all_to_all | solution.py:94
  26.4 1.9 %collective-permute-start.1 = (f32[10,1,4,128]{3,2,1,0:T(4,128)S(1)}, f32[10,1,4,128]{3,2,1,0:T(4,128)S(1)}, u32[]{:S(2)}, u32[]{:S(2)}) collective-permute-start(f32[10,1,4,128]{3,2,1,0:T(4,128)S(1)} %get-tuple-element.218), channel_id=1, source_target_pairs={{0,64},{64,128},{128,192},{192,256},{256,320},{320,384},{384,448},... | collective-permute-start | bytes 61448 | tf_op jit(solution)/shard_map/ppermute | solution.py:27
  28.3 4.9 %collective-permute-start = (f32[10,1,4,128]{3,2,1,0:T(4,128)S(1)}, f32[10,1,4,128]{3,2,1,0:T(4,128)S(1)}, u32[]{:S(2)}, u32[]{:S(2)}) collective-permute-start(f32[10,1,4,128]{3,2,1,0:T(4,128)S(1)} %get-tuple-element.217), channel_id=1, source_target_pairs={{64,0},{128,64},{192,128},{256,192},{320,256},{384,320},{448,384},... | collective-permute-start | bytes 61448 | tf_op jit(solution)/shard_map/ppermute | solution.py:29
  33.2 0.1 fusion.81
  33.3 5.2 %all-to-all-done = s32[64,2,128]{2,1,0:T(2,128)S(1)} async-done(((s32[64,2,128]{2,1,0:T(2,128)}), s32[64,2,128]{2,1,0:T(2,128)S(1)}, u32[]{:S(2)}, u32[]{:S(2)}) %all-to-all-start) | async-done | bytes 65568 | tf_op jit(solution)/shard_map/all_to_all | solution.py:94
  38.6 23.3 %while.29 = (s32[]{:T(128)}, f32[8,2048]{1,0:T(8,128)S(1)}, f32[8,2048]{1,0:T(8,128)S(1)}, s32[8,2048]{1,0:T(8,128)S(1)}, f32[128,16]{0,1:T(8,128)S(1)}, /*index=5*/s32[]{:T(128)}, s32[]{:T(128)}) while((s32[]{:T(128)}, f32[8,2048]{1,0:T(8,128)S(1)}, f32[8,2048]{1,0:T(8,128)S(1)}, s32[8,2048]{1,0:T(8,128)S(1)}, f32[128,16]{0,1:T(8,128)S(1)}, ...), condition=%wide.region_6.7_spmd, body=%wide.region_3.6_spmd.sunk | while | flops 50987008 | bytes 391257 | solution.py:113
  38.7 2.4 %fusion.93 = f32[2048,16]{0,1:T(8,128)S(1)} fusion(f32[128,16]{0,1:T(8,128)S(1)} %get-tuple-element.323, s32[2048]{0:T(1024)S(1)} %get-tuple-element.290, pred[2048]{0:T(1024)(128)(4,1)S(1)} %broadcast_compare_fusion.4), kind=kOutput, calls=%fused_computation.7.clone.1 | convolution fusion | flops 50855936 | bytes 149504 | tf_op jit(solution)/shard_map/while/body/eval_jaxpr/dot_general | solution.py:103
  41.1 0.2 dynamic_update_slice.16
  41.3 0.2 dynamic_update_slice.15
  41.6 2.4 %fusion.93 = f32[2048,16]{0,1:T(8,128)S(1)} fusion(f32[128,16]{0,1:T(8,128)S(1)} %get-tuple-element.323, s32[2048]{0:T(1024)S(1)} %get-tuple-element.290, pred[2048]{0:T(1024)(128)(4,1)S(1)} %broadcast_compare_fusion.4), kind=kOutput, calls=%fused_computation.7.clone.1 | convolution fusion | flops 50855936 | bytes 149504 | tf_op jit(solution)/shard_map/while/body/eval_jaxpr/dot_general | solution.py:103
  44.0 0.2 dynamic_update_slice.16
  44.2 0.2 dynamic_update_slice.15
  44.5 2.4 %fusion.93 = f32[2048,16]{0,1:T(8,128)S(1)} fusion(f32[128,16]{0,1:T(8,128)S(1)} %get-tuple-element.323, s32[2048]{0:T(1024)S(1)} %get-tuple-element.290, pred[2048]{0:T(1024)(128)(4,1)S(1)} %broadcast_compare_fusion.4), kind=kOutput, calls=%fused_computation.7.clone.1 | convolution fusion | flops 50855936 | bytes 149504 | tf_op jit(solution)/shard_map/while/body/eval_jaxpr/dot_general | solution.py:103
  46.9 0.2 dynamic_update_slice.16
  47.1 0.2 dynamic_update_slice.15
  47.4 2.4 %fusion.93 = f32[2048,16]{0,1:T(8,128)S(1)} fusion(f32[128,16]{0,1:T(8,128)S(1)} %get-tuple-element.323, s32[2048]{0:T(1024)S(1)} %get-tuple-element.290, pred[2048]{0:T(1024)(128)(4,1)S(1)} %broadcast_compare_fusion.4), kind=kOutput, calls=%fused_computation.7.clone.1 | convolution fusion | flops 50855936 | bytes 149504 | tf_op jit(solution)/shard_map/while/body/eval_jaxpr/dot_general | solution.py:103
  49.8 0.2 dynamic_update_slice.16
  50.0 0.2 dynamic_update_slice.15
  50.3 2.4 %fusion.93 = f32[2048,16]{0,1:T(8,128)S(1)} fusion(f32[128,16]{0,1:T(8,128)S(1)} %get-tuple-element.323, s32[2048]{0:T(1024)S(1)} %get-tuple-element.290, pred[2048]{0:T(1024)(128)(4,1)S(1)} %broadcast_compare_fusion.4), kind=kOutput, calls=%fused_computation.7.clone.1 | convolution fusion | flops 50855936 | bytes 149504 | tf_op jit(solution)/shard_map/while/body/eval_jaxpr/dot_general | solution.py:103
  52.7 0.2 dynamic_update_slice.16
  53.0 0.2 dynamic_update_slice.15
  53.2 2.4 %fusion.93 = f32[2048,16]{0,1:T(8,128)S(1)} fusion(f32[128,16]{0,1:T(8,128)S(1)} %get-tuple-element.323, s32[2048]{0:T(1024)S(1)} %get-tuple-element.290, pred[2048]{0:T(1024)(128)(4,1)S(1)} %broadcast_compare_fusion.4), kind=kOutput, calls=%fused_computation.7.clone.1 | convolution fusion | flops 50855936 | bytes 149504 | tf_op jit(solution)/shard_map/while/body/eval_jaxpr/dot_general | solution.py:103
  55.7 0.2 dynamic_update_slice.16
  55.9 0.2 dynamic_update_slice.15
  56.1 2.4 %fusion.93 = f32[2048,16]{0,1:T(8,128)S(1)} fusion(f32[128,16]{0,1:T(8,128)S(1)} %get-tuple-element.323, s32[2048]{0:T(1024)S(1)} %get-tuple-element.290, pred[2048]{0:T(1024)(128)(4,1)S(1)} %broadcast_compare_fusion.4), kind=kOutput, calls=%fused_computation.7.clone.1 | convolution fusion | flops 50855936 | bytes 149504 | tf_op jit(solution)/shard_map/while/body/eval_jaxpr/dot_general | solution.py:103
  58.6 0.2 dynamic_update_slice.16
  58.8 0.2 dynamic_update_slice.15
  59.1 2.4 %fusion.93 = f32[2048,16]{0,1:T(8,128)S(1)} fusion(f32[128,16]{0,1:T(8,128)S(1)} %get-tuple-element.323, s32[2048]{0:T(1024)S(1)} %get-tuple-element.290, pred[2048]{0:T(1024)(128)(4,1)S(1)} %broadcast_compare_fusion.4), kind=kOutput, calls=%fused_computation.7.clone.1 | convolution fusion | flops 50855936 | bytes 149504 | tf_op jit(solution)/shard_map/while/body/eval_jaxpr/dot_general | solution.py:103
  61.5 0.2 dynamic_update_slice.16
  61.7 0.2 dynamic_update_slice.15
  61.9 0.7 reshape.259
  62.6 7.5 %all-to-all-start.1 = ((f32[64,2,128]{2,1,0:T(2,128)}), f32[64,2,128]{2,1,0:T(2,128)S(1)}, u32[]{:S(2)}, u32[]{:S(2)}) async-start(f32[64,2,128]{2,1,0:T(2,128)} %reshape.259), calls=%async_computation.1 | async-start | bytes 131072 | tf_op jit(solution)/shard_map/all_to_all | solution.py:115
  70.2 0.7 reshape.261
  70.9 11.5 %all-to-all-done.1 = f32[64,2,128]{2,1,0:T(2,128)S(1)} async-done(((f32[64,2,128]{2,1,0:T(2,128)}), f32[64,2,128]{2,1,0:T(2,128)S(1)}, u32[]{:S(2)}, u32[]{:S(2)}) %all-to-all-start.1) | async-done | bytes 65568 | tf_op jit(solution)/shard_map/all_to_all | solution.py:115
  82.3 4.6 %all-to-all-start.2 = ((f32[64,2,128]{2,1,0:T(2,128)}), f32[64,2,128]{2,1,0:T(2,128)S(1)}, u32[]{:S(2)}, u32[]{:S(2)}) async-start(f32[64,2,128]{2,1,0:T(2,128)} %reshape.261), calls=%async_computation.2 | async-start | bytes 131072 | tf_op jit(solution)/shard_map/all_to_all | solution.py:116
  87.0 1.3 collective-permute-start.2
  88.3 4.5 %collective-permute-start.3 = (f32[10,4,1,128]{3,2,1,0:T(1,128)S(1)}, f32[10,4,1,128]{3,2,1,0:T(1,128)S(1)}, u32[]{:S(2)}, u32[]{:S(2)}) collective-permute-start(f32[10,4,1,128]{3,2,1,0:T(1,128)S(1)} %get-tuple-element.212), channel_id=1, source_target_pairs={{0,1},{1,2},{2,3},{3,4},{4,5},{5,6},{6,7},{7,8},{8,9},{9,10},{10,1... | collective-permute-start | bytes 61448 | tf_op jit(solution)/shard_map/ppermute | solution.py:27
  92.8 0.6 gather_fusion
  93.4 5.7 %all-to-all-done.2 = f32[64,2,128]{2,1,0:T(2,128)S(1)} async-done(((f32[64,2,128]{2,1,0:T(2,128)}), f32[64,2,128]{2,1,0:T(2,128)S(1)}, u32[]{:S(2)}, u32[]{:S(2)}) %all-to-all-start.2) | async-done | bytes 65568 | tf_op jit(solution)/shard_map/all_to_all | solution.py:116
  99.2 0.6 gather_fusion.1
  99.7 0.1 copy-done.1
  99.9 1.3 scatter_custom_fusion.2
  101.2 7.1 %all-to-all-start.4 = ((f32[64,2,128]{2,1,0:T(2,128)}), f32[64,2,128]{2,1,0:T(2,128)S(1)}, u32[]{:S(2)}, u32[]{:S(2)}) async-start(f32[64,2,128]{2,1,0:T(2,128)} %bitcast.14), calls=%async_computation.4 | async-start | bytes 131072 | tf_op jit(solution)/shard_map/all_to_all | solution.py:122
  108.4 0.1 fusion.27
  108.5 1.4 scatter_custom_fusion.1
  109.9 10.7 %all-to-all-done.4 = f32[64,2,128]{2,1,0:T(2,128)S(1)} async-done(((f32[64,2,128]{2,1,0:T(2,128)}), f32[64,2,128]{2,1,0:T(2,128)S(1)}, u32[]{:S(2)}, u32[]{:S(2)}) %all-to-all-start.4) | async-done | bytes 65568 | tf_op jit(solution)/shard_map/all_to_all | solution.py:122
  120.6 4.6 %all-to-all-start.3 = ((f32[64,2,128]{2,1,0:T(2,128)}), f32[64,2,128]{2,1,0:T(2,128)S(1)}, u32[]{:S(2)}, u32[]{:S(2)}) async-start(f32[64,2,128]{2,1,0:T(2,128)} %bitcast.13), calls=%async_computation.3 | async-start | bytes 131072 | tf_op jit(solution)/shard_map/all_to_all | solution.py:121
  125.2 0.7 add_select_fusion.2
  126.0 11.5 %all-to-all-done.3 = f32[64,2,128]{2,1,0:T(2,128)S(1)} async-done(((f32[64,2,128]{2,1,0:T(2,128)}), f32[64,2,128]{2,1,0:T(2,128)S(1)}, u32[]{:S(2)}, u32[]{:S(2)}) %all-to-all-start.3) | async-done | bytes 65568 | tf_op jit(solution)/shard_map/all_to_all | solution.py:121
  137.6 7.9 %while.30 = (s32[]{:T(128)}, f32[16,128]{1,0:T(8,128)S(1)}, s32[8,2048]{1,0:T(8,128)S(1)}, f32[8,2048]{1,0:T(8,128)S(1)}, f32[8,2048]{1,0:T(8,128)S(1)}, /*index=5*/s32[]{:T(128)}, s32[]{:T(128)}) while((s32[]{:T(128)}, f32[16,128]{1,0:T(8,128)S(1)}, s32[8,2048]{1,0:T(8,128)S(1)}, f32[8,2048]{1,0:T(8,128)S(1)}, ...), condition=%wide.region_10.11_spmd.clone, body=%wide.region_9.10_spmd.clone.sunk | while | flops 50995200 | bytes 399455 | solution.py:144
  137.7 0.9 convolution_add_fusion.2
  138.7 0.9 convolution_add_fusion.2
  139.7 0.9 convolution_add_fusion.2
  140.7 0.9 convolution_add_fusion.2
  141.6 0.9 convolution_add_fusion.2
  142.6 0.9 convolution_add_fusion.2
  143.6 0.9 convolution_add_fusion.2
  144.6 0.9 convolution_add_fusion.2
  145.5 0.6 copy-done.3
  (109 shorter events, 1.7 us)
Async XLA Ops:
  0.6 0.7 copy-start.8
  1.4 0.7 copy-start.4
  1.6 0.7 copy-start.5
  3.6 22.8 %copy-start = (f32[10,2,4,128]{3,2,1,0:T(4,128)S(1)}, f32[10,2,4,128]{3,2,1,0:T(4,128)}, u32[]{:S(2)}) copy-start(f32[10,2,4,128]{3,2,1,0:T(4,128)} %param.16) | copy-start | bytes 122884
  3.6 35.0 %all-to-all-start = ((s32[64,2,128]{2,1,0:T(2,128)}), s32[64,2,128]{2,1,0:T(2,128)S(1)}, u32[]{:S(2)}, u32[]{:S(2)}) async-start(s32[64,2,128]{2,1,0:T(2,128)} %bitcast.6), calls=%async_computation | async-start | bytes 131072 | tf_op jit(solution)/shard_map/all_to_all | solution.py:94
  26.4 6.9 %collective-permute-start.1 = (f32[10,1,4,128]{3,2,1,0:T(4,128)S(1)}, f32[10,1,4,128]{3,2,1,0:T(4,128)S(1)}, u32[]{:S(2)}, u32[]{:S(2)}) collective-permute-start(f32[10,1,4,128]{3,2,1,0:T(4,128)S(1)} %get-tuple-element.218), channel_id=1, source_target_pairs={{0,64},{64,128},{128,192},{192,256},{256,320},{320,384},{384,448},... | collective-permute-start | bytes 61448 | tf_op jit(solution)/shard_map/ppermute | solution.py:27
  28.3 41.8 %collective-permute-start = (f32[10,1,4,128]{3,2,1,0:T(4,128)S(1)}, f32[10,1,4,128]{3,2,1,0:T(4,128)S(1)}, u32[]{:S(2)}, u32[]{:S(2)}) collective-permute-start(f32[10,1,4,128]{3,2,1,0:T(4,128)S(1)} %get-tuple-element.217), channel_id=1, source_target_pairs={{64,0},{128,64},{192,128},{256,192},{320,256},{384,320},{448,384},... | collective-permute-start | bytes 61448 | tf_op jit(solution)/shard_map/ppermute | solution.py:29
  62.6 19.7 %all-to-all-start.1 = ((f32[64,2,128]{2,1,0:T(2,128)}), f32[64,2,128]{2,1,0:T(2,128)S(1)}, u32[]{:S(2)}, u32[]{:S(2)}) async-start(f32[64,2,128]{2,1,0:T(2,128)} %reshape.259), calls=%async_computation.1 | async-start | bytes 131072 | tf_op jit(solution)/shard_map/all_to_all | solution.py:115
  82.3 16.8 %all-to-all-start.2 = ((f32[64,2,128]{2,1,0:T(2,128)}), f32[64,2,128]{2,1,0:T(2,128)S(1)}, u32[]{:S(2)}, u32[]{:S(2)}) async-start(f32[64,2,128]{2,1,0:T(2,128)} %reshape.261), calls=%async_computation.2 | async-start | bytes 131072 | tf_op jit(solution)/shard_map/all_to_all | solution.py:116
  87.0 21.4 %collective-permute-start.2 = (f32[10,4,1,128]{3,2,1,0:T(1,128)S(1)}, f32[10,4,1,128]{3,2,1,0:T(1,128)S(1)}, u32[]{:S(2)}, u32[]{:S(2)}) collective-permute-start(f32[10,4,1,128]{3,2,1,0:T(1,128)S(1)} %get-tuple-element.211), channel_id=1, source_target_pairs={{1,0},{2,1},{3,2},{4,3},{5,4},{6,5},{7,6},{8,7},{9,8},{10,9},{11,1... | collective-permute-start | bytes 61448 | tf_op jit(solution)/shard_map/ppermute | solution.py:29
  88.3 20.1 %collective-permute-start.3 = (f32[10,4,1,128]{3,2,1,0:T(1,128)S(1)}, f32[10,4,1,128]{3,2,1,0:T(1,128)S(1)}, u32[]{:S(2)}, u32[]{:S(2)}) collective-permute-start(f32[10,4,1,128]{3,2,1,0:T(1,128)S(1)} %get-tuple-element.212), channel_id=1, source_target_pairs={{0,1},{1,2},{2,3},{3,4},{4,5},{5,6},{6,7},{7,8},{8,9},{9,10},{10,1... | collective-permute-start | bytes 61448 | tf_op jit(solution)/shard_map/ppermute | solution.py:27
  99.2 0.7 copy-start.1
  99.2 0.7 copy-start.2
  101.2 7.1 %copy-start.6 = (f32[2,4,128]{2,1,0:T(4,128)S(1)}, f32[2,4,128]{2,1,0:T(4,128)}, u32[]{:S(2)}) copy-start(f32[2,4,128]{2,1,0:T(4,128)} %param.18) | copy-start | bytes 12292
  101.2 7.1 %copy-start.7 = (f32[2,4,128]{2,1,0:T(4,128)S(1)}, f32[2,4,128]{2,1,0:T(4,128)}, u32[]{:S(2)}) copy-start(f32[2,4,128]{2,1,0:T(4,128)} %param.17) | copy-start | bytes 12292
  101.2 19.4 %all-to-all-start.4 = ((f32[64,2,128]{2,1,0:T(2,128)}), f32[64,2,128]{2,1,0:T(2,128)S(1)}, u32[]{:S(2)}, u32[]{:S(2)}) async-start(f32[64,2,128]{2,1,0:T(2,128)} %bitcast.14), calls=%async_computation.4 | async-start | bytes 131072 | tf_op jit(solution)/shard_map/all_to_all | solution.py:122
  120.6 16.9 %all-to-all-start.3 = ((f32[64,2,128]{2,1,0:T(2,128)}), f32[64,2,128]{2,1,0:T(2,128)S(1)}, u32[]{:S(2)}, u32[]{:S(2)}) async-start(f32[64,2,128]{2,1,0:T(2,128)} %bitcast.13), calls=%async_computation.3 | async-start | bytes 131072 | tf_op jit(solution)/shard_map/all_to_all | solution.py:121
  145.5 0.6 copy-start.3
where the time goes:
time: 147 us; the launch traced here: 146 us
  starting transfers between devices  59.1 us (40%)
  waiting for transfers between devices  44.7 us (30%)
  matrix products  25.7 us (17%)
  local copies, waits for them, and re-layouts  8.52 us (6%)
  other arithmetic  6.14 us (4%)
    all_to_all x1, starting transfers between devices, body(): lax.all_to_all(to_slots(sent_cell, -1), 'yz', split_axis=0, concat_axis=0...  22.7 us
    dot_general x8, matrix products, one_block(): jnp.dot(lower_hot, both_tables, precision=lax.Precision.HIGHEST, preferre...  18.9 us
    all_to_all x1, waiting for transfers between devices, body(): lax.all_to_all(fuel_gas, 'yz', split_axis=0, concat_axis=0, tiled=True)  11.5 us
    all_to_all x1, waiting for transfers between devices, body(): lax.all_to_all(to_slots(src_mass, 0.0), 'yz', split_axis=0, concat_axis=0...  11.5 us
    all_to_all x1, waiting for transfers between devices, body(): lax.all_to_all(to_slots(src_energy, 0.0), 'yz', split_axis=0, concat_axis...  10.7 us
    all_to_all x1, starting transfers between devices, body(): lax.all_to_all(fuel_gas, 'yz', split_axis=0, concat_axis=0, tiled=True)  7.48 us
    all_to_all x1, starting transfers between devices, body(): lax.all_to_all(to_slots(src_energy, 0.0), 'yz', split_axis=0, concat_axis...  7.1 us
    dot_general x8, matrix products, add_block(): lax.dot_general(weighted, lower_hot, (((0,), (0,)), ((), ())), precision=...  6.84 us
  transfers between devices with their start and end apart: 9, of which 5 were waited for; matrix products, arithmetic and copies ran while one was open for 20% of the time, Pallas kernels for 0%

commit v1 on v0

v1 whole, which is shorter than its diff:
```python
import functools
import math

import jax
import jax.numpy as jnp
from jax import lax
from jax.experimental import pallas as pl
from jax.experimental.pallas import tpu as pltpu
from jax.sharding import PartitionSpec as P

SUBSTEPS = 4
evap_coef = 0.3
heat_coef = 0.8
latent_coef = 0.5
drop_dt = 0.25

MESH = pl.DeviceIdType.MESH
LANES = 128
SUB = 8
SLOTS = 2
ROWS = 3 * SLOTS
F32 = jnp.float32
BF16 = jnp.bfloat16


def split3(value):
    high = value.astype(BF16)
    rest = value - high.astype(F32)
    middle = rest.astype(BF16)
    low = (rest - middle.astype(F32)).astype(BF16)
    return high, middle, low


def softplus(x):
    return jnp.maximum(x, 0.0) + jnp.log1p(jnp.exp(-jnp.abs(x)))


def droplet_step(mass_now, temp_now, fuel_gas, temp_gas):
    src_mass = jnp.zeros_like(mass_now)
    src_energy = jnp.zeros_like(mass_now)
    for substep in range(SUBSTEPS):
        evap_rate = evap_coef * softplus(temp_now - fuel_gas)
        heat_flow = heat_coef * (temp_gas - temp_now)
        shrunk = mass_now * jnp.exp(-drop_dt * evap_rate)
        src_mass = src_mass + (mass_now - shrunk)
        src_energy = src_energy - drop_dt * heat_flow * mass_now
        temp_now = temp_now + drop_dt * (heat_flow - latent_coef * evap_rate)
        mass_now = shrunk
    return mass_now, temp_now, src_mass, src_energy


def kernel(
    n_gx, side,
    gas_hbm, kappa_hbm, vel_hbm, mass_hbm, temp_hbm, fill_hbm, cell_hbm, dest_hbm,
    gas_out, mass_out, temp_out,
    gas, kappa, vel, mass, temp, fill, cell, dest, dest_s,
    tables, outgo, relay, arrive, halo_x, halo_y, own_gas,
    in_sem, ready_z, ready_x, ready_d,
    gp_send, dp_send, g1_send, g1_recv, d1_send, d1_recv, g2_send, g2_recv, d2_send, d2_recv, halo_send, halo_recv,
):
    n_yz = side * side
    gx = lax.axis_index("gx")
    me = lax.axis_index("yz")
    me_x, me_z = me // side, me % side
    nfield = gas.shape[0]
    blocks = mass.shape[0]
    half = SUB // 2
    has_xm, has_xp = gx > 0, gx < n_gx - 1
    has_ym, has_yp = me > 0, me < n_yz - 1
    wrap_up = jnp.logical_and(me_z == side - 1, has_yp)
    wrap_down = jnp.logical_and(me_z == 0, has_ym)

    one = jnp.int32(1)
    zero = jnp.int32(0)

    late_z = jnp.where(jnp.logical_and(gx == 0, me_x == 0), one, zero)
    late_x = jnp.where(jnp.logical_and(gx == 0, me_z == 0), one, zero)
    is_late = jnp.logical_and(gx == 0, me == 0)
    past_corner = jnp.logical_and(jnp.logical_and(gx == 0, me_x == 0), me_z > 0)
    by_corner = jnp.logical_and(jnp.logical_and(gx == 0, me_z == 0), me_x > 0)

    def rank_z(z):
        late = jnp.where(z == 0, side - 2, jnp.where(z == side - 1, side - 1, z - 1))
        return jnp.where(late_z == 1, late, z)

    def turn_z(t):
        late = jnp.where(t == side - 2, 0, jnp.where(t == side - 1, side - 1, t + 1))
        return jnp.where(is_late, t, jnp.where(late_z == 1, late, t))

    def rank_x(x):
        return (jnp.where(x < side // 2, x, side // 2 + side - 1 - x) + side - late_x) % side

    my_rank = rank_x(me_x)
    my_turn = rank_z(me_z)

    def signal(sem, where):
        pl.semaphore_signal(sem, inc=1, device_id=where, device_id_type=MESH)

    loads = [
        pltpu.make_async_copy(src, dst, in_sem.at[i])
        for i, (src, dst) in enumerate(
            (
                (gas_hbm.at[0], tables.at[me_z, me_x, 0]),
                (gas_hbm.at[nfield - 1], tables.at[me_z, me_x, 1]),
                (dest_hbm, dest), (fill_hbm, fill), (cell_hbm, cell), (mass_hbm, mass),
                (temp_hbm, temp), (dest_hbm, dest_s),
                (gas_hbm, gas), (kappa_hbm, kappa), (vel_hbm, vel),
            )
        )
    ]
    for load in loads:
        load.start()

    halo_x[...] = jnp.zeros_like(halo_x)
    halo_y[...] = jnp.zeros_like(halo_y)

    barrier = pltpu.get_barrier_semaphore()

    def greet_z(z, carry):
        @pl.when(rank_z(z) > my_turn)
        def _():
            signal(barrier, {"yz": me_x * side + z})

        return carry

    def greet_x(x, carry):
        @pl.when(rank_x(x) > my_rank)
        def _():
            signal(barrier, {"yz": x * side + me_z})

        return carry

    lax.fori_loop(0, side, greet_z, 0)
    lax.fori_loop(0, side, greet_x, 0)

    @pl.when(by_corner)
    def _():
        def greet(z, carry):
            signal(barrier, {"yz": z})
            return carry

        lax.fori_loop(1, side, greet, 0)

    @pl.when(has_xm)
    def _():
        signal(barrier, {"gx": gx - 1})

    @pl.when(has_xp)
    def _():
        signal(barrier, {"gx": gx + 1})

    @pl.when(wrap_down)
    def _():
        signal(barrier, {"yz": me - 1})

    pl.semaphore_wait(
        barrier,
        my_turn + my_rank + jnp.where(has_xm, one, zero) + jnp.where(has_xp, one, zero)
        + jnp.where(wrap_up, one, zero) + jnp.where(past_corner, side - 1, 0),
    )
    for load in loads[:2]:
        load.wait()

    def remote(src, dst, send_sem, recv_sem, where):
        return pltpu.make_async_remote_copy(
            src_ref=src, dst_ref=dst, send_sem=send_sem, recv_sem=recv_sem,
            device_id=where, device_id_type=MESH,
        )

    def kinds(z):
        return pl.ds(z * ROWS, ROWS)

    def gas_along_z(z):
        mine = tables.at[me_z, me_x]
        return remote(mine, mine, g1_send, g1_recv.at[me_z], {"yz": me_x * side + z})

    def drops_along_z(z):
        return remote(outgo.at[kinds(z)], relay.at[kinds(me_z)], d1_send, d1_recv.at[me_z], {"yz": me_x * side + z})

    def gas_along_x(z, x):
        tile = tables.at[z, me_x]
        return remote(tile, tile, g2_send, g2_recv.at[z], {"yz": x * side + me_z})

    def drops_along_x(z, x):
        return remote(
            relay.at[kinds(z), x], arrive.at[kinds(z), me_x],
            d2_send, d2_recv.at[z], {"yz": x * side + me_z},
        )

    def early_gas(z, carry):
        @pl.when(rank_z(z) < my_turn)
        def _():
            gas_along_z(z).start()

        return carry

    lax.fori_loop(0, side, early_gas, 0)

    def gas_past(x):
        tile = tables.at[me_z, me_x]
        return remote(tile, tile, gp_send, g2_recv.at[me_z], {"yz": x * side})

    def drops_past(x):
        return remote(
            outgo.at[kinds(0), x], arrive.at[kinds(me_z), me_x], dp_send, d2_recv.at[me_z], {"yz": x * side}
        )

    def past(make):
        @pl.when(past_corner)
        def _():
            def send(x, carry):
                make(x).start()
                return carry

            lax.fori_loop(1, side, send, 0)

    past(gas_past)

    def tell_z(z, carry):
        @pl.when(rank_z(z) < my_turn)
        def _():
            signal(ready_z.at[me_z], {"yz": me_x * side + z})

        return carry

    def tell_x(x, carry):
        @pl.when(rank_x(x) < my_rank)
        def _():
            signal(ready_x.at[me_x], {"yz": x * side + me_z})

        return carry

    lax.fori_loop(0, side, tell_z, 0)
    lax.fori_loop(0, side, tell_x, 0)

    @pl.when(wrap_up)
    def _():
        signal(ready_d, {"yz": me + 1})


    for load in loads[2:8]:
        load.wait()
    row_i = lax.broadcasted_iota(jnp.int32, (blocks, blocks), 0)
    col_i = lax.broadcasted_iota(jnp.int32, (blocks, blocks), 1)
    dest_row = jnp.broadcast_to(dest[...], (blocks, blocks)).astype(F32)
    fill_row = jnp.broadcast_to(fill[...], (blocks, blocks)).astype(F32)
    dest_col = jnp.sum(jnp.where(row_i == col_i, dest_row, 0.0), axis=1, keepdims=True)
    fill_col = jnp.sum(jnp.where(row_i == col_i, fill_row, 0.0), axis=1, keepdims=True)
    same = jnp.where(dest_row == dest_col, 1.0, 0.0)
    rank_row = jnp.sum(jnp.where(row_i < col_i, same, 0.0), axis=0, keepdims=True)
    swapped_dest = (dest[...] % side) * side + dest[...] // side
    slot_row = rank_row * n_yz + swapped_dest.astype(F32)
    total = SLOTS * n_yz
    pick_slot = jnp.where(
        lax.broadcasted_iota(jnp.int32, (total, blocks), 0).astype(F32) == slot_row, 1.0, 0.0
    ).astype(BF16)
    lane = lax.broadcasted_iota(jnp.int32, (blocks, LANES), 1).astype(F32)
    living = lane < fill_col
    code = jnp.where(living, cell[...] + 1, 0).astype(F32)
    packed = jnp.concatenate([mass[...], temp[...], code], axis=1)
    placed = sum(
        jnp.dot(pick_slot, part, preferred_element_type=F32) for part in split3(packed)
    )
    for kind in range(3):
        for slot in range(SLOTS):
            for z in range(side):
                start = slot * n_yz + z * side
                outgo[z * ROWS + kind * SLOTS + slot] = placed[
                    start : start + side, kind * LANES : (kind + 1) * LANES
                ]

    def early_drops(z, carry):
        @pl.when(rank_z(z) < my_turn)
        def _():
            drops_along_z(z).start()

        return carry

    lax.fori_loop(0, side, early_drops, 0)
    past(drops_past)

    for load in loads[8:]:
        load.wait()

    def halo_copy(src, dst, index, where):
        return remote(src, dst, halo_send.at[index], halo_recv.at[index], where)

    to_xp = [halo_copy(gas.at[:, half:SUB], halo_x.at[:, 0:half], 0, {"gx": gx + 1})]
    to_xm = [halo_copy(gas.at[:, 0:half], halo_x.at[:, half:SUB], 1, {"gx": gx - 1})]
    to_yp = [
        halo_copy(gas.at[:, pl.ds(g + half - 1, 1)], halo_y.at[:, pl.ds(g, 1)], 2 + i, {"yz": me + 1})
        for i, g in enumerate((0, half))
    ]
    to_ym = [
        halo_copy(gas.at[:, pl.ds(g, 1)], halo_y.at[:, pl.ds(g + half - 1, 1)], 4 + i, {"yz": me - 1})
        for i, g in enumerate((0, half))
    ]

    def start_if(condition, copies):
        @pl.when(condition)
        def _():
            for copy in copies:
                copy.start()

    start_if(has_xp, to_xp)
    start_if(has_xm, to_xm)
    start_if(wrap_up, to_yp)
    up_z, down_z = me_z < side - 1, me_z > 0
    start_if(jnp.logical_and(up_z, rank_z(me_z + 1) < my_turn), to_yp)
    start_if(jnp.logical_and(down_z, rank_z(me_z - 1) < my_turn), to_ym)
    relay[kinds(me_z)] = outgo[kinds(me_z)]

    def await_x(x, carry):
        @pl.when(jnp.logical_and(rank_x(x) > my_rank, jnp.logical_not(jnp.logical_and(by_corner, x == 0))))
        def _():
            pl.semaphore_wait(ready_x.at[x], 1)

        return carry

    lax.fori_loop(0, side, await_x, 0)

    def step_on(z):
        @pl.when(rank_z(z) > my_turn)
        def _():
            pl.semaphore_wait(ready_z.at[z], 1)
            gas_along_z(z).start()
            drops_along_z(z).start()

        start_if(jnp.logical_and(z == me_z + 1, rank_z(z) > my_turn), to_yp)
        start_if(jnp.logical_and(z == me_z - 1, rank_z(z) > my_turn), to_ym)

        @pl.when(z != me_z)
        def _():
            remote(
                tables.at[z, me_x], tables.at[z, me_x], g1_send, g1_recv.at[z], {"yz": me}
            ).wait_recv()

        relays = jnp.logical_or(jnp.logical_not(is_late), z == me_z)
        first = jnp.where(by_corner, one, zero)

        def forward_gas(x, carry):
            @pl.when(jnp.logical_and(x != me_x, relays))
            def _():
                gas_along_x(z, x).start()

            return carry

        lax.fori_loop(first, side, forward_gas, 0)

        @pl.when(z != me_z)
        def _():
            remote(relay.at[kinds(z)], relay.at[kinds(z)], d1_send, d1_recv.at[z], {"yz": me}).wait_recv()

        def forward_drops(x, carry):
            @pl.when(jnp.logical_and(x != me_x, relays))
            def _():
                drops_along_x(z, x).start()

            return carry

        lax.fori_loop(first, side, forward_drops, 0)
        arrive[kinds(z), pl.ds(me_x, 1), :] = relay[kinds(z), pl.ds(me_x, 1), :]

    def bulk(view, sem):
        return pltpu.make_async_copy(view, view, sem)

    row_ids = lax.broadcasted_iota(jnp.int32, (LANES, LANES), 0)
    up_rows = lax.broadcasted_iota(jnp.int32, (SUB, LANES), 0)

    def group_in(z):
        bulk(arrive.at[kinds(z), pl.ds(0, side - 1)], d2_recv.at[z]).wait()

        def kind_of(kind):
            return jnp.concatenate(
                [
                    arrive[z * ROWS + kind * SLOTS + slot]
                    for slot in range(SLOTS)
                ],
                axis=0,
            )

        mass_in, temp_in = kind_of(0), kind_of(1)
        place = kind_of(2).astype(jnp.int32) - 1
        lower = place & (LANES - 1)
        upper = place >> 7
        fuel_gas = jnp.zeros_like(mass_in)
        temp_gas = jnp.zeros_like(mass_in)
        fuel_field = tables[me_z, me_x, 0]
        temp_field = tables[me_z, me_x, 1]
        for u in range(SUB):
            here = upper == u
            fuel_row = jnp.broadcast_to(fuel_field[u : u + 1], mass_in.shape)
            temp_row = jnp.broadcast_to(temp_field[u : u + 1], mass_in.shape)
            fuel_gas = jnp.where(
                here, jnp.take_along_axis(fuel_row, lower, axis=1, mode="promise_in_bounds"), fuel_gas
            )
            temp_gas = jnp.where(
                here, jnp.take_along_axis(temp_row, lower, axis=1, mode="promise_in_bounds"), temp_gas
            )
        return mass_in, temp_in, fuel_gas, temp_gas, lower, upper

    def deposit(lower, upper, src_mass, src_energy):
        values = []
        for value in (src_mass, src_energy):
            high = value.astype(BF16).astype(F32)
            values += [high, value - high]
        hots, weighted = [], []
        for b in range(lower.shape[0]):
            hots.append(jnp.where(lower[b : b + 1] == row_ids, 1.0, 0.0).astype(BF16))
            here = upper[b : b + 1] == up_rows
            weighted.append(
                jnp.concatenate([jnp.where(here, v[b : b + 1], 0.0) for v in values], axis=0).astype(BF16)
            )
        return lax.dot_general(
            jnp.concatenate(weighted, axis=1), jnp.concatenate(hots, axis=1),
            (((1,), (1,)), ((), ())), preferred_element_type=F32,
        )

    def group(z):
        mass_in, temp_in, fuel_gas, temp_gas, lower, upper = group_in(z)
        _, _, src_mass, src_energy = droplet_step(mass_in, temp_in, fuel_gas, temp_gas)
        return deposit(lower, upper, src_mass, src_energy)

    def gas_ready(z):
        bulk(tables.at[z, pl.ds(0, side - 1)], g2_recv.at[z]).wait()

    def advance(t, carry):
        step_on(turn_z(t))
        return carry

    lax.fori_loop(0, side, advance, 0)

    summed = lax.fori_loop(
        0, side - 1, lambda z, summed: summed + group(z), jnp.zeros((4 * SUB, LANES), F32)
    )

    @pl.when(wrap_down)
    def _():
        pl.semaphore_wait(ready_d, 1)
        for copy in to_ym:
            copy.start()

    for exists, copies in ((has_xm, to_xp), (has_xp, to_xm), (has_ym, to_yp), (has_yp, to_ym)):

        @pl.when(exists)
        def _(copies=copies):
            for copy in copies:
                copy.wait_recv()

    sub_id = lax.broadcasted_iota(jnp.int32, (SUB, LANES), 0)
    lane_id = lax.broadcasted_iota(jnp.int32, (SUB, LANES), 1)
    first_x = sub_id < half
    first_y, last_y = sub_id % half == 0, sub_id % half == half - 1
    first_z, last_z = lane_id == 0, lane_id == LANES - 1
    kap, velo = kappa[...], vel[...]
    ends = {}
    for f in range(nfield):
        field, hx, hy = gas[f], halo_x[f], halo_y[f]
        swapped = pltpu.roll(field, half, 0)
        before_x = jnp.where(first_x, hx, swapped)
        after_x = jnp.where(first_x, swapped, hx)
        before_y = jnp.where(first_y, hy, pltpu.roll(field, 1, 0))
        after_y = jnp.where(last_y, hy, pltpu.roll(field, SUB - 1, 0))
        before_z = jnp.where(first_z, field, pltpu.roll(field, 1, 1))
        after_z = jnp.where(last_z, field, pltpu.roll(field, LANES - 1, 1))
        beside = after_x + before_x + after_y + before_y + after_z + before_z
        moved = field + kap * (beside - 6.0 * field) - velo * (field - before_x)
        if f in (0, nfield - 1):
            ends[f] = moved
        else:
            gas_out[f] = moved

    @pl.when(by_corner)
    def _():
        pl.semaphore_wait(ready_x.at[0], 1)

        def forward(z, carry):
            gas_along_x(z, 0).start()
            drops_along_x(z, 0).start()
            return carry

        lax.fori_loop(0, side, forward, 0)

    for z in range(side):
        gas_ready(z)
    for j in range(blocks):
        target = dest_s[0, j]
        z, x = target % side, target // side
        place = cell[pl.ds(j, 1), :]
        lower = jnp.broadcast_to(place & (LANES - 1), (SUB, LANES))
        here = (place >> 7) == up_rows
        for kind in range(2):
            looked = jnp.take_along_axis(tables[z, x, kind], lower, axis=1, mode="promise_in_bounds")
            own_gas[kind, pl.ds(j, 1), :] = jnp.sum(jnp.where(here, looked, 0.0), axis=0, keepdims=True)
    mass_in, temp_in, fuel_gas, temp_gas, lower, upper = group_in(side - 1)
    _, _, src_mass, src_energy = droplet_step(mass_in, temp_in, fuel_gas, temp_gas)
    own_mass, own_temp, _, _ = droplet_step(mass[...], temp[...], own_gas[0], own_gas[1])
    mass_out[...] = jnp.where(living, own_mass, 0.0)
    temp_out[...] = jnp.where(living, own_temp, 0.0)
    summed = summed + deposit(lower, upper, src_mass, src_energy)
    gas_out[0] = ends[0] + (summed[0:SUB] + summed[SUB : 2 * SUB])
    gas_out[nfield - 1] = ends[nfield - 1] + (summed[2 * SUB : 3 * SUB] + summed[3 * SUB : 4 * SUB])

    bulk(tables.at[0, pl.ds(0, side - 1)], g1_send).wait()
    bulk(outgo.at[pl.ds(0, (side - 1) * ROWS)], d1_send).wait()

    @pl.when(is_late)
    def _():
        bulk(tables.at[0, pl.ds(0, side - 1)], g2_send).wait()
        bulk(arrive.at[kinds(0), pl.ds(0, side - 1)], d2_send).wait()

    @pl.when(jnp.logical_not(is_late))
    def _():
        bulk(tables.at[pl.ds(0, side - 1)], g2_send).wait()
        bulk(arrive.at[:, pl.ds(0, side - 1)], d2_send).wait()

    @pl.when(past_corner)
    def _():
        bulk(tables.at[0, pl.ds(0, side - 1)], gp_send).wait()
        bulk(arrive.at[kinds(0), pl.ds(0, side - 1)], dp_send).wait()

    for exists, copies in ((has_xp, to_xp), (has_xm, to_xm), (has_yp, to_yp), (has_ym, to_ym)):

        @pl.when(exists)
        def _(copies=copies):
            for copy in copies:
                copy.wait_send()


def solution(mesh):
    n_gx, n_yz = mesh.shape["gx"], mesh.shape["yz"]
    side = math.isqrt(n_yz)
    assert side * side == n_yz

    def body(gas, kappa, velocity, drop_mass, drop_temp, block_fill, drop_cell, block_dest):
        nfield, cx, cy, cz = gas.shape
        blocks = drop_mass.shape[0]
        any_spec = pl.BlockSpec(memory_space=pl.ANY)
        vmem_spec = pl.BlockSpec(memory_space=pltpu.VMEM)
        tile = (cx * cy, cz)
        dma = pltpu.SemaphoreType.DMA
        regular = pltpu.SemaphoreType.REGULAR
        gas_next, mass_next, temp_next = pl.pallas_call(
            functools.partial(kernel, n_gx, side),
            out_shape=(
                pltpu.VMEM((nfield,) + tile, F32),
                pltpu.VMEM(drop_mass.shape, F32),
                pltpu.VMEM(drop_mass.shape, F32),
            ),
            in_specs=[any_spec] * 8,
            out_specs=(vmem_spec,) * 3,
            scratch_shapes=[
                pltpu.VMEM((nfield,) + tile, F32),
                pltpu.VMEM(tile, F32),
                pltpu.VMEM(tile, F32),
                pltpu.VMEM((blocks, LANES), F32),
                pltpu.VMEM((blocks, LANES), F32),
                pltpu.VMEM((1, blocks), jnp.int32),
                pltpu.VMEM((blocks, LANES), jnp.int32),
                pltpu.VMEM((1, blocks), jnp.int32),
                pltpu.SMEM((1, blocks), jnp.int32),
                pltpu.VMEM((side, side, 2) + tile, F32),
                pltpu.VMEM((side * ROWS, side, LANES), F32),
                pltpu.VMEM((side * ROWS, side, LANES), F32),
                pltpu.VMEM((side * ROWS, side, LANES), F32),
                pltpu.VMEM((nfield,) + tile, F32),
                pltpu.VMEM((nfield,) + tile, F32),
                pltpu.VMEM((2, blocks, LANES), F32),
                dma((11,)),
                regular((side,)),
                regular((side,)),
                regular,
                dma, dma,
                dma, dma((side,)), dma, dma((side,)),
                dma, dma((side,)), dma, dma((side,)),
                dma((6,)), dma((6,)),
            ],
            compiler_params=pltpu.CompilerParams(collective_id=0, has_side_effects=True),
            name="spray_step",
        )(
            gas.reshape((nfield,) + tile),
            kappa.reshape(tile),
            velocity.reshape(tile),
            drop_mass,
            drop_temp,
            block_fill.reshape(1, blocks),
            drop_cell,
            block_dest.reshape(1, blocks),
        )
        return gas_next.reshape(gas.shape), mass_next, temp_next

    in_specs = (
        P(None, "gx", "yz", None),
        P("gx", "yz", None),
        P("gx", "yz", None),
        P(("gx", "yz"), None),
        P(("gx", "yz"), None),
        P(("gx", "yz")),
        P(("gx", "yz"), None),
        P(("gx", "yz"), None),
    )
    out_specs = (P(None, "gx", "yz", None), P(("gx", "yz"), None), P(("gx", "yz"), None))
    return jax.shard_map(body, mesh=mesh, in_specs=in_specs, out_specs=out_specs, check_vma=False)
```

time: 147 us -> 36.2 us (0.25)
  the two profiles are of different devices: /device:TPU:64 before, /device:TPU:2 now
where the time goes in v1:
time: 36.2 us; the launch traced here: 36 us
  Pallas kernels  33.6 us (93%)
  local copies, waits for them, and re-layouts  1.83 us (5%)
  between operations  0.64 us (2%)
    pallas_call x1, Pallas kernels, body(): pl.pallas_call(functools.partial(kernel, n_gx, side), out_shape=(pltpu.VM...  33.6 us
    unnamed x3, local copies, waits for them, and re-layouts  1.83 us

profile of v1, /device:TPU:2, one launch (start us, length us, event | category | flops | bytes accessed | tf_op | source)
XLA Modules:
  0.0 36.0 jit_solution(14375002057919026831)
XLA Ops:
  0.6 33.6 %spray_step.1 = (f32[10,8,128]{2,1,0:T(8,128)S(1)}, f32[32,128]{1,0:T(8,128)S(1)}, f32[32,128]{1,0:T(8,128)S(1)}) custom-call(f32[10,8,128]{2,1,0:T(8,128)} %bitcast.7, f32[8,128]{1,0:T(8,128)} %bitcast.8, f32[8,128]{1,0:T(8,128)} %bitcast.9, f32[32,128]{1,0:T(8,128)} %mass_hbm.1, f32[32,128]{1,0:T(8,128)} %temp_hbm.1, s32[1,32]{1,0:T(1,128)} %bitcast.10, ...), custom_call_target="tpu_custom_call" | custom-call | tf_op jit(solution)/shard_map/spray_step/pallas_call | solution.py:543
  34.2 0.6 %copy.14 = f32[10,2,4,128]{3,2,1,0:T(4,128)} copy(f32[10,2,4,128]{3,2,1,0:T(4,128)S(1)} %bitcast.6) | data formatting | bytes 81920
  34.8 0.6 %copy.15 = f32[32,128]{1,0:T(8,128)} copy(f32[32,128]{1,0:T(8,128)S(1)} %get-tuple-element.10) | data formatting | bytes 32768
  35.4 0.6 %copy.16 = f32[32,128]{1,0:T(8,128)} copy(f32[32,128]{1,0:T(8,128)S(1)} %get-tuple-element.11) | data formatting | bytes 32768

commit v2 on v1

--- a/solution.py
+++ b/solution.py
@@ -54,7 +54,7 @@
     gas_hbm, kappa_hbm, vel_hbm, mass_hbm, temp_hbm, fill_hbm, cell_hbm, dest_hbm,
     gas_out, mass_out, temp_out,
     gas, kappa, vel, mass, temp, fill, cell, dest, dest_s,
-    tables, outgo, relay, arrive, halo_x, halo_y, own_gas,
+    tables, outgo, relay, arrive, halo_x, halo_y, picked,
     in_sem, ready_z, ready_x, ready_d,
     gp_send, dp_send, g1_send, g1_recv, d1_send, d1_recv, g2_send, g2_recv, d2_send, d2_recv, halo_send, halo_recv,
 ):
@@ -486,12 +486,18 @@
     for j in range(blocks):
         target = dest_s[0, j]
         z, x = target % side, target // side
-        place = cell[pl.ds(j, 1), :]
-        lower = jnp.broadcast_to(place & (LANES - 1), (SUB, LANES))
-        here = (place >> 7) == up_rows
         for kind in range(2):
-            looked = jnp.take_along_axis(tables[z, x, kind], lower, axis=1, mode="promise_in_bounds")
-            own_gas[kind, pl.ds(j, 1), :] = jnp.sum(jnp.where(here, looked, 0.0), axis=0, keepdims=True)
+            picked[kind, pl.ds(j * SUB, SUB), :] = tables[z, x, kind]
+    own_lower = cell[...] & (LANES - 1)
+    own_upper = cell[...] >> 7
+    own_gas = []
+    for kind in range(2):
+        found = jnp.zeros((blocks, LANES), F32)
+        for u in range(SUB):
+            row = picked[kind, pl.ds(u, blocks, stride=SUB), :]
+            looked = jnp.take_along_axis(row, own_lower, axis=1, mode="promise_in_bounds")
+            found = jnp.where(own_upper == u, looked, found)
+        own_gas.append(found)
     mass_in, temp_in, fuel_gas, temp_gas, lower, upper = group_in(side - 1)
     _, _, src_mass, src_energy = droplet_step(mass_in, temp_in, fuel_gas, temp_gas)
     own_mass, own_temp, _, _ = droplet_step(mass[...], temp[...], own_gas[0], own_gas[1])
@@ -525,6 +531,17 @@
         def _(copies=copies):
             for copy in copies:
                 copy.wait_send()
+
+
+def emit(gas_in, mass_in, temp_in, gas_out, mass_out, temp_out, sems):
+    copies = [
+        pltpu.make_async_copy(src, dst, sems.at[i])
+        for i, (src, dst) in enumerate(((gas_in, gas_out), (mass_in, mass_out), (temp_in, temp_out)))
+    ]
+    for copy in copies:
+        copy.start()
+    for copy in copies:
+        copy.wait()
 
 
 def solution(mesh):
@@ -565,7 +582,7 @@
                 pltpu.VMEM((side * ROWS, side, LANES), F32),
                 pltpu.VMEM((nfield,) + tile, F32),
                 pltpu.VMEM((nfield,) + tile, F32),
-                pltpu.VMEM((2, blocks, LANES), F32),
+                pltpu.VMEM((2, blocks * SUB, LANES), F32),
                 dma((11,)),
                 regular((side,)),
                 regular((side,)),
@@ -587,6 +604,18 @@
             drop_cell,
             block_dest.reshape(1, blocks),
         )
+        gas_next, mass_next, temp_next = pl.pallas_call(
+            emit,
+            out_shape=(
+                jax.ShapeDtypeStruct((nfield,) + tile, F32),
+                jax.ShapeDtypeStruct(drop_mass.shape, F32),
+                jax.ShapeDtypeStruct(drop_mass.shape, F32),
+            ),
+            in_specs=(vmem_spec,) * 3,
+            out_specs=(any_spec,) * 3,
+            scratch_shapes=[dma((3,))],
+            name="emit",
+        )(*(pltpu.with_memory_space_constraint(a, pltpu.VMEM) for a in (gas_next, mass_next, temp_next)))
         return gas_next.reshape(gas.shape), mass_next, temp_next
 
     in_specs = (

time: 36.2 us -> 35 us (0.967)
  local copies, waits for them, and re-layouts: 1.83 us -> 0 us
  Pallas kernels: 33.6 us -> 34.2 us
    unnamed x3 -> x0, local copies, waits for them, and re-layouts: 1.83 us -> none
    pallas_call x0 -> x1, Pallas kernels: none -> 0.65 us  [body(): pl.pallas_call(emit, out_shape=(jax.ShapeDtypeStruct((nfield,) + tile, F3...]
where the time goes in v2:
time: 35 us; the launch traced here: 34.9 us
  Pallas kernels  34.2 us (98%)
  between operations  0.64 us (2%)
    pallas_call x1, Pallas kernels, body(): pl.pallas_call(functools.partial(kernel, n_gx, side), out_shape=(pltpu.VM...  33.6 us

profile of v2, /device:TPU:2, one launch (start us, length us, event | category | flops | bytes accessed | tf_op | source)
XLA Modules:
  0.0 34.9 jit_solution(16828051947412672286)
XLA Ops:
  0.6 33.6 %spray_step.1 = (f32[10,8,128]{2,1,0:T(8,128)S(1)}, f32[32,128]{1,0:T(8,128)S(1)}, f32[32,128]{1,0:T(8,128)S(1)}) custom-call(f32[10,8,128]{2,1,0:T(8,128)} %bitcast.6, f32[8,128]{1,0:T(8,128)} %bitcast.7, f32[8,128]{1,0:T(8,128)} %bitcast.8, f32[32,128]{1,0:T(8,128)} %mass_hbm.1, f32[32,128]{1,0:T(8,128)} %temp_hbm.1, s32[1,32]{1,0:T(1,128)} %bitcast.9, ...), custom_call_target="tpu_custom_call" | custom-call | tf_op jit(solution)/shard_map/spray_step/pallas_call | solution.py:560
  34.2 0.7 %emit.1 = (f32[10,8,128]{2,1,0:T(8,128)}, f32[32,128]{1,0:T(8,128)}, f32[32,128]{1,0:T(8,128)}) custom-call(f32[10,8,128]{2,1,0:T(8,128)S(1)} %get-tuple-element.9.gas_in, f32[32,128]{1,0:T(8,128)S(1)} %get-tuple-element.10.mass_in, f32[32,128]{1,0:T(8,128)S(1)} %get-tuple-element.11.temp_in), custom_call_target="tpu_custom_call" | custom-call | tf_op jit(solution)/shard_map/emit/pallas_call | solution.py:607

commit v3 on v2

--- a/solution.py
+++ b/solution.py
@@ -116,6 +116,14 @@
 
     barrier = pltpu.get_barrier_semaphore()
 
+    @pl.when(has_xm)
+    def _():
+        signal(barrier, {"gx": gx - 1})
+
+    @pl.when(has_xp)
+    def _():
+        signal(barrier, {"gx": gx + 1})
+
     def greet_z(z, carry):
         @pl.when(rank_z(z) > my_turn)
         def _():
@@ -141,102 +149,9 @@
 
         lax.fori_loop(1, side, greet, 0)
 
-    @pl.when(has_xm)
-    def _():
-        signal(barrier, {"gx": gx - 1})
-
-    @pl.when(has_xp)
-    def _():
-        signal(barrier, {"gx": gx + 1})
-
     @pl.when(wrap_down)
     def _():
         signal(barrier, {"yz": me - 1})
-
-    pl.semaphore_wait(
-        barrier,
-        my_turn + my_rank + jnp.where(has_xm, one, zero) + jnp.where(has_xp, one, zero)
-        + jnp.where(wrap_up, one, zero) + jnp.where(past_corner, side - 1, 0),
-    )
-    for load in loads[:2]:
-        load.wait()
-
-    def remote(src, dst, send_sem, recv_sem, where):
-        return pltpu.make_async_remote_copy(
-            src_ref=src, dst_ref=dst, send_sem=send_sem, recv_sem=recv_sem,
-            device_id=where, device_id_type=MESH,
-        )
-
-    def kinds(z):
-        return pl.ds(z * ROWS, ROWS)
-
-    def gas_along_z(z):
-        mine = tables.at[me_z, me_x]
-        return remote(mine, mine, g1_send, g1_recv.at[me_z], {"yz": me_x * side + z})
-
-    def drops_along_z(z):
-        return remote(outgo.at[kinds(z)], relay.at[kinds(me_z)], d1_send, d1_recv.at[me_z], {"yz": me_x * side + z})
-
-    def gas_along_x(z, x):
-        tile = tables.at[z, me_x]
-        return remote(tile, tile, g2_send, g2_recv.at[z], {"yz": x * side + me_z})
-
-    def drops_along_x(z, x):
-        return remote(
-            relay.at[kinds(z), x], arrive.at[kinds(z), me_x],
-            d2_send, d2_recv.at[z], {"yz": x * side + me_z},
-        )
-
-    def early_gas(z, carry):
-        @pl.when(rank_z(z) < my_turn)
-        def _():
-            gas_along_z(z).start()
-
-        return carry
-
-    lax.fori_loop(0, side, early_gas, 0)
-
-    def gas_past(x):
-        tile = tables.at[me_z, me_x]
-        return remote(tile, tile, gp_send, g2_recv.at[me_z], {"yz": x * side})
-
-    def drops_past(x):
-        return remote(
-            outgo.at[kinds(0), x], arrive.at[kinds(me_z), me_x], dp_send, d2_recv.at[me_z], {"yz": x * side}
-        )
-
-    def past(make):
-        @pl.when(past_corner)
-        def _():
-            def send(x, carry):
-                make(x).start()
-                return carry
-
-            lax.fori_loop(1, side, send, 0)
-
-    past(gas_past)
-
-    def tell_z(z, carry):
-        @pl.when(rank_z(z) < my_turn)
-        def _():
-            signal(ready_z.at[me_z], {"yz": me_x * side + z})
-
-        return carry
-
-    def tell_x(x, carry):
-        @pl.when(rank_x(x) < my_rank)
-        def _():
-            signal(ready_x.at[me_x], {"yz": x * side + me_z})
-
-        return carry
-
-    lax.fori_loop(0, side, tell_z, 0)
-    lax.fori_loop(0, side, tell_x, 0)
-
-    @pl.when(wrap_up)
-    def _():
-        signal(ready_d, {"yz": me + 1})
-
 
     for load in loads[2:8]:
         load.wait()
@@ -269,6 +184,69 @@
                     start : start + side, kind * LANES : (kind + 1) * LANES
                 ]
 
+    pl.semaphore_wait(
+        barrier,
+        my_turn + my_rank + jnp.where(has_xm, one, zero) + jnp.where(has_xp, one, zero)
+        + jnp.where(wrap_up, one, zero) + jnp.where(past_corner, side - 1, 0),
+    )
+    for load in loads[:2]:
+        load.wait()
+
+    def remote(src, dst, send_sem, recv_sem, where):
+        return pltpu.make_async_remote_copy(
+            src_ref=src, dst_ref=dst, send_sem=send_sem, recv_sem=recv_sem,
+            device_id=where, device_id_type=MESH,
+        )
+
+    def kinds(z):
+        return pl.ds(z * ROWS, ROWS)
+
+    def gas_along_z(z):
+        mine = tables.at[me_z, me_x]
+        return remote(mine, mine, g1_send, g1_recv.at[me_z], {"yz": me_x * side + z})
+
+    def drops_along_z(z):
+        return remote(outgo.at[kinds(z)], relay.at[kinds(me_z)], d1_send, d1_recv.at[me_z], {"yz": me_x * side + z})
+
+    def gas_along_x(z, x):
+        tile = tables.at[z, me_x]
+        return remote(tile, tile, g2_send, g2_recv.at[z], {"yz": x * side + me_z})
+
+    def drops_along_x(z, x):
+        return remote(
+            relay.at[kinds(z), x], arrive.at[kinds(z), me_x],
+            d2_send, d2_recv.at[z], {"yz": x * side + me_z},
+        )
+
+    def early_gas(z, carry):
+        @pl.when(rank_z(z) < my_turn)
+        def _():
+            gas_along_z(z).start()
+
+        return carry
+
+    lax.fori_loop(0, side, early_gas, 0)
+
+    def gas_past(x):
+        tile = tables.at[me_z, me_x]
+        return remote(tile, tile, gp_send, g2_recv.at[me_z], {"yz": x * side})
+
+    def drops_past(x):
+        return remote(
+            outgo.at[kinds(0), x], arrive.at[kinds(me_z), me_x], dp_send, d2_recv.at[me_z], {"yz": x * side}
+        )
+
+    def past(make):
+        @pl.when(past_corner)
+        def _():
+            def send(x, carry):
+                make(x).start()
+                return carry
+
+            lax.fori_loop(1, side, send, 0)
+
+    past(gas_past)
+
     def early_drops(z, carry):
         @pl.when(rank_z(z) < my_turn)
         def _():
@@ -278,6 +256,28 @@
 
     lax.fori_loop(0, side, early_drops, 0)
     past(drops_past)
+
+    def tell_z(z, carry):
+        @pl.when(rank_z(z) < my_turn)
+        def _():
+            signal(ready_z.at[me_z], {"yz": me_x * side + z})
+
+        return carry
+
+    def tell_x(x, carry):
+        @pl.when(rank_x(x) < my_rank)
+        def _():
+            signal(ready_x.at[me_x], {"yz": x * side + me_z})
+
+        return carry
+
+    lax.fori_loop(0, side, tell_z, 0)
+    lax.fori_loop(0, side, tell_x, 0)
+
+    @pl.when(wrap_up)
+    def _():
+        signal(ready_d, {"yz": me + 1})
+
 
     for load in loads[8:]:
         load.wait()
@@ -319,15 +319,18 @@
 
     lax.fori_loop(0, side, await_x, 0)
 
-    def step_on(z):
-        @pl.when(rank_z(z) > my_turn)
+    def send_to(z, above):
+        @pl.when(rank_z(z) > above)
         def _():
             pl.semaphore_wait(ready_z.at[z], 1)
             gas_along_z(z).start()
             drops_along_z(z).start()
 
-        start_if(jnp.logical_and(z == me_z + 1, rank_z(z) > my_turn), to_yp)
-        start_if(jnp.logical_and(z == me_z - 1, rank_z(z) > my_turn), to_ym)
+        start_if(jnp.logical_and(z == me_z + 1, rank_z(z) > above), to_yp)
+        start_if(jnp.logical_and(z == me_z - 1, rank_z(z) > above), to_ym)
+
+    def step_on(z):
+        send_to(z, my_turn + 2)
 
         @pl.when(z != me_z)
         def _():
@@ -424,8 +427,29 @@
     def gas_ready(z):
         bulk(tables.at[z, pl.ds(0, side - 1)], g2_recv.at[z]).wait()
 
+    def to_corner(z, carry):
+        gas_along_x(z, 0).start()
+        drops_along_x(z, 0).start()
+        return carry
+
+    for ahead in (1, 2):
+
+        @pl.when(my_turn + ahead < side)
+        def _(ahead=ahead):
+            send_to(turn_z(my_turn + ahead), my_turn)
+
     def advance(t, carry):
         step_on(turn_z(t))
+
+        @pl.when(jnp.logical_and(by_corner, t == side - 2))
+        def _():
+            pl.semaphore_wait(ready_x.at[0], 1)
+            lax.fori_loop(0, side - 1, to_corner, 0)
+
+        @pl.when(jnp.logical_and(by_corner, t == side - 1))
+        def _():
+            to_corner(side - 1, 0)
+
         return carry
 
     lax.fori_loop(0, side, advance, 0)
@@ -469,17 +493,6 @@
             ends[f] = moved
         else:
             gas_out[f] = moved
-
-    @pl.when(by_corner)
-    def _():
-        pl.semaphore_wait(ready_x.at[0], 1)
-
-        def forward(z, carry):
-            gas_along_x(z, 0).start()
-            drops_along_x(z, 0).start()
-            return carry
-
-        lax.fori_loop(0, side, forward, 0)
 
     for z in range(side):
         gas_ready(z)

time: 35 us -> 34.3 us (0.980)
  the two profiles are of different devices: /device:TPU:2 before, /device:TPU:689 now
where the time goes in v3:
time: 34.3 us; the launch traced here: 34.1 us
  Pallas kernels  33.5 us (98%)
  between operations  0.64 us (2%)
    pallas_call x1, Pallas kernels, body(): pl.pallas_call(functools.partial(kernel, n_gx, side), out_shape=(pltpu.VM...  32.8 us

profile of v3, /device:TPU:689, one launch (start us, length us, event | category | flops | bytes accessed | tf_op | source)
XLA Modules:
  0.0 34.1 jit_solution(1057872924974713291)
XLA Ops:
  0.6 32.8 %spray_step.1 = (f32[10,8,128]{2,1,0:T(8,128)S(1)}, f32[32,128]{1,0:T(8,128)S(1)}, f32[32,128]{1,0:T(8,128)S(1)}) custom-call(f32[10,8,128]{2,1,0:T(8,128)} %bitcast.6, f32[8,128]{1,0:T(8,128)} %bitcast.7, f32[8,128]{1,0:T(8,128)} %bitcast.8, f32[32,128]{1,0:T(8,128)} %mass_hbm.1, f32[32,128]{1,0:T(8,128)} %temp_hbm.1, s32[1,32]{1,0:T(1,128)} %bitcast.9, ...), custom_call_target="tpu_custom_call" | custom-call | tf_op jit(solution)/shard_map/spray_step/pallas_call | solution.py:573
  33.4 0.7 %emit.1 = (f32[10,8,128]{2,1,0:T(8,128)}, f32[32,128]{1,0:T(8,128)}, f32[32,128]{1,0:T(8,128)}) custom-call(f32[10,8,128]{2,1,0:T(8,128)S(1)} %get-tuple-element.9.gas_in, f32[32,128]{1,0:T(8,128)S(1)} %get-tuple-element.10.mass_in, f32[32,128]{1,0:T(8,128)S(1)} %get-tuple-element.11.temp_in), custom_call_target="tpu_custom_call" | custom-call | tf_op jit(solution)/shard_map/emit/pallas_call | solution.py:620
